TPU v7x, 32 devices: a whole 2x2x4 slice. The times are simulated.
32 devices in a mesh: seq: 8 (over z, core), tp: 4 (over y, x).
Axes of the slice: x: 2, y: 2, z: 4, core: 2. Of those that a mesh axis runs over, the one named last changes fastest.
Arguments:
- tokens: bfloat16 [64, 6144], P('seq'), may hold values from -6 to 6
- out_grad: bfloat16 [64, 6144], P('seq'), may hold values from -1.5 to 1.5
- w_in: bfloat16 [6144, 24576], P('seq', 'tp'), may hold values from -0.078125 to 0.078125
- w_out: bfloat16 [24576, 6144], P('tp', 'seq'), may hold values from -0.0390625 to 0.0390625
Outputs:
- input_grad: bfloat16 [64, 6144], P('tp', 'seq')
- grad_in: float32 [6144, 24576], P('seq', 'tp')
- grad_out: float32 [24576, 6144], P('tp', 'seq')
All inputs are finite; a program needn't handle non-finite values.
Results may differ from a plain program's by a relative error of at most 0.0051.
Values may be sent and summed in bfloat16 or wider, within the bound.
A program may use at most 128 MiB of HBM per device.

v0:
```python
import jax
import jax.numpy as jnp
from jax import lax
from jax.sharding import PartitionSpec as P


def over_rows(left, right):
    return lax.dot_general(
        left, right, (((0,), (0,)), ((), ())), preferred_element_type=jnp.float32
    )


def over_cols(left, right):
    return lax.dot_general(
        left, right, (((1,), (1,)), ((), ())), preferred_element_type=jnp.float32
    )


def per_device(tokens, out_grad, w_in, w_out):
    cols_x, cols_dy = (
        lax.all_to_all(tokens, "seq", split_axis=1, concat_axis=0, tiled=True),
        lax.all_to_all(out_grad, "seq", split_axis=1, concat_axis=0, tiled=True),
    )
    pre = jnp.dot(cols_x, w_in, preferred_element_type=jnp.float32)
    hidden_grad = over_cols(cols_dy, w_out)
    pre_share, grad_share = (
        lax.psum_scatter(pre, "seq", scatter_dimension=0, tiled=True),
        lax.psum_scatter(hidden_grad, "seq", scatter_dimension=0, tiled=True),
    )
    posit = jnp.maximum(pre_share, 0.0)
    act = (posit * posit).astype(jnp.bfloat16)
    slope = (2.0 * posit * grad_share).astype(jnp.bfloat16)
    act_piece = lax.all_gather(act, "seq", axis=0, tiled=True)
    slope_piece = lax.all_gather(slope, "seq", axis=0, tiled=True)
    sum_out = over_rows(act_piece, cols_dy)
    sum_in = over_rows(cols_x, slope_piece)
    partial_value = over_cols(slope_piece, w_in)
    grad_in, grad_out, partial_value = (sum_in, sum_out, partial_value)
    input_grad = lax.psum_scatter(partial_value, "tp", scatter_dimension=0, tiled=True).astype(
        jnp.bfloat16
    )
    return (input_grad, grad_in, grad_out)


def solution(mesh):
    return jax.shard_map(
        per_device,
        mesh=mesh,
        in_specs=(P("seq", None), P("seq", None), P("seq", "tp"), P("tp", "seq")),
        out_specs=(P("tp", "seq"), P("seq", "tp"), P("tp", "seq")),
        check_vma=False,
    )
```

profile of v0, /device:TPU:0, one launch (start us, length us, event | category | flops | bytes accessed | tf_op | source)
XLA Modules:
  0.0 180.2 jit_solution(3376550464443689663)
XLA Ops:
  7.2 0.0 reduce-scatter.6.cloned.1.call-start
  7.2 12.7 %all_to_all.38 = bf16[8,8,768]{2,0,1:T(8,128)(2,1)S(1)} all-to-all(bf16[8,8,768]{2,0,1:T(8,128)(2,1)} %bitcast.24), channel_id=1, replica_groups=mesh['seq'=8,'tp'=4] {'seq'}, dimensions={1} | all-to-all | bytes 196608 | tf_op jit(solution)/shard_map/all_to_all | solution.py:22
  19.9 0.0 copy-start
  19.9 7.8 %fusion.2 = f32[64,6144]{1,0:T(8,128)} fusion(bf16[6144,768]{1,0:T(8,128)(2,1)} %param.7, bf16[8,8,768]{2,0,1:T(8,128)(2,1)S(1)} %all_to_all.38), kind=kOutput, calls=%fused_computation.5 | convolution fusion | flops 603979776 | bytes 11108352 | tf_op jit(solution)/shard_map/dot_general | solution.py:14
  27.7 0.0 reduce-scatter.6.cloned.1.call-update
  27.7 0.0 reduce-scatter.4.cloned.1.call-start
  27.8 0.0 copy-done
  27.8 8.8 %all_to_all.39 = bf16[8,8,768]{2,0,1:T(8,128)(2,1)S(1)} all-to-all(bf16[8,8,768]{2,0,1:T(8,128)(2,1)S(1)} %bitcast.25), channel_id=1, replica_groups=mesh['seq'=8,'tp'=4] {'seq'}, dimensions={1} | all-to-all | bytes 196608 | tf_op jit(solution)/shard_map/all_to_all | solution.py:21
  36.6 6.6 %fusion.5 = f32[64,6144]{1,0:T(8,128)} fusion(bf16[768,6144]{1,0:T(8,128)(2,1)} %param.6, bf16[8,8,768]{2,0,1:T(8,128)(2,1)S(1)} %all_to_all.39), kind=kOutput, calls=%fused_computation.8 | convolution fusion | flops 603979776 | bytes 11108352 | tf_op jit(solution)/shard_map/dot_general | solution.py:24
  43.2 0.0 reduce-scatter.4.cloned.1.call-update
  43.2 0.0 reduce-scatter.8.cloned.1.call-start
  43.3 17.8 %reduce-scatter.6.cloned.1.call-done = f32[8,6144]{1,0:T(8,128)} async-done(((f32[64,6144]{1,0:T(8,128)}), f32[8,6144]{1,0:T(8,128)}) %reduce-scatter.6.cloned.1.call-update) | async-done | bytes 196624 | tf_op jit(solution)/shard_map/reduce_scatter | solution.py:28
  61.0 35.5 %reduce-scatter.4.cloned.1.call-done = f32[8,6144]{1,0:T(8,128)} async-done(((f32[64,6144]{1,0:T(8,128)}), f32[8,6144]{1,0:T(8,128)}) %reduce-scatter.4.cloned.1.call-update) | async-done | bytes 196624 | tf_op jit(solution)/shard_map/reduce_scatter | solution.py:27
  96.6 1.1 multiply_convert_fusion
  97.6 15.8 %all_gather.7 = bf16[64,6144]{1,0:T(8,128)(2,1)S(1)} all-gather(bf16[8,6144]{1,0:T(8,128)(2,1)S(1)} %get-tuple-element.6), channel_id=1, replica_groups=mesh['seq'=8,'tp'=4] {'seq'}, dimensions={0}, use_global_device_ids=true | all-gather | bytes 884736 | tf_op jit(solution)/shard_map/all_gather | solution.py:33
  113.4 16.2 %all_gather.6 = bf16[64,6144]{1,0:T(8,128)(2,1)S(1)} all-gather(bf16[8,6144]{1,0:T(8,128)(2,1)S(1)} %get-tuple-element.7), channel_id=1, replica_groups=mesh['seq'=8,'tp'=4] {'seq'}, dimensions={0}, use_global_device_ids=true | all-gather | bytes 884736 | tf_op jit(solution)/shard_map/all_gather | solution.py:34
  129.6 7.3 %fusion.7 = f32[64,768]{1,0:T(8,128)} fusion(bf16[64,6144]{1,0:T(8,128)(2,1)S(1)} %all_gather.6, bf16[768,6144]{1,0:T(8,128)(2,1)} %param.6), kind=kOutput, calls=%fused_computation.10 | convolution fusion | flops 603979776 | bytes 10420224 | tf_op jit(solution)/shard_map/dot_general | solution.py:14
  136.9 0.0 reduce-scatter.8.cloned.1.call-update
  137.0 8.3 %convolution_bitcast_fusion = f32[768,6144]{0,1:T(8,128)} fusion(bf16[64,6144]{1,0:T(8,128)(2,1)S(1)} %all_gather.6, bf16[8,8,768]{2,0,1:T(8,128)(2,1)S(1)} %all_to_all.39), kind=kOutput, calls=%fused_computation | convolution fusion | flops 603979776 | bytes 19759104 | tf_op jit(solution)/shard_map/dot_general | solution.py:8
  145.3 18.7 %copy.7 = f32[768,6144]{1,0:T(8,128)} copy(f32[768,6144]{0,1:T(8,128)} %convolution_bitcast_fusion) | data formatting | bytes 37748736
  164.0 8.3 %fusion = f32[6144,768]{1,0:T(8,128)} fusion(bf16[64,6144]{1,0:T(8,128)(2,1)S(1)} %all_gather.7, bf16[8,8,768]{2,0,1:T(8,128)(2,1)S(1)} %all_to_all.38), kind=kOutput, calls=%fused_computation.3 | convolution fusion | flops 603979776 | bytes 19759104 | tf_op jit(solution)/shard_map/dot_general | solution.py:8
  172.2 0.0 reduce-scatter.8.cloned.1.call-done
  172.2 1.4 convert_element_type.10
Async XLA Ops:
  7.2 53.9 %reduce-scatter.6.cloned.1.call-start = ((), (), s32[]{:S(2)}) async-start(), calls=%async_computation.6 | async-start | bytes 1769472 | tf_op jit(solution)/shard_map/reduce_scatter | solution.py:28
  19.9 7.9 %copy-start = (bf16[8,6144]{1,0:T(8,128)(2,1)S(1)}, bf16[8,6144]{1,0:T(8,128)(2,1)}, u32[]{:S(2)}) copy-start(bf16[8,6144]{1,0:T(8,128)(2,1)} %param.4) | copy-start | bytes 294916
  27.7 68.9 %reduce-scatter.4.cloned.1.call-start = ((), (), s32[]{:S(2)}) async-start(), calls=%async_computation.5 | async-start | bytes 1769472 | tf_op jit(solution)/shard_map/reduce_scatter | solution.py:27
  43.2 129.0 %reduce-scatter.8.cloned.1.call-start = ((), (), s32[]{:S(2)}) async-start(), calls=%async_computation.7 | async-start | bytes 245760 | tf_op jit(solution)/shard_map/reduce_scatter | solution.py:39
Sparse Core Ops, SparseCore 0:
  27.8 33.1 reduce-scatter.5
  63.9 32.6 reduce-scatter.3
  137.1 21.8 reduce-scatter.7
where the time goes:
time: 181 us; the launch traced here: 180 us
  blocking collectives  53.5 us (30%)
  waiting for transfers between devices  53.3 us (29%)
  matrix products  38.3 us (21%)
  local copies, waits for them, and re-layouts  18.7 us (10%)
  between operations  13.8 us (8%)
  other arithmetic  2.47 us (1%)
    reduce_scatter x1, waiting for transfers between devices, per_device(): lax.psum_scatter(pre, 'seq', scatter_dimension=0, tiled=True)  35.5 us
    unnamed x3, local copies, waits for them, and re-layouts  18.7 us
    reduce_scatter x1, waiting for transfers between devices, per_device(): lax.psum_scatter(hidden_grad, 'seq', scatter_dimension=0, tiled=True)  17.8 us
    dot_general x2, matrix products, over_rows(): lax.dot_general(left, right, (((0,), (0,)), ((), ())), preferred_element_...  16.6 us
    all_gather x1, blocking collectives, per_device(): slope_piece = lax.all_gather(slope, 'seq', axis=0, tiled=True)  16.2 us
    all_gather x1, blocking collectives, per_device(): act_piece = lax.all_gather(act, 'seq', axis=0, tiled=True)  15.8 us
    dot_general x2, matrix products, over_cols(): lax.dot_general(left, right, (((1,), (1,)), ((), ())), preferred_element_...  15.1 us
    all_to_all x1, blocking collectives, per_device(): lax.all_to_all(out_grad, 'seq', split_axis=1, concat_axis=0, tiled=True)  12.7 us
  transfers between devices with their start and end apart: 3, of which 2 were waited for; matrix products, arithmetic and copies ran while one was open for 23% of the time, Pallas kernels for 0%

commit v1 on v0

v1 whole, which is shorter than its diff:
```python
import functools

import jax
import jax.numpy as jnp
from jax import lax
from jax.experimental import pallas as pl
from jax.experimental.pallas import tpu as pltpu
from jax.sharding import PartitionSpec as P

CHUNKS = 12
LAG = 2
F32 = jnp.float32
BF16 = jnp.bfloat16


def remote(src, dst, send_sem, recv_sem, axis, target):
    return pltpu.make_async_remote_copy(
        src_ref=src,
        dst_ref=dst,
        send_sem=send_sem,
        recv_sem=recv_sem,
        device_id={axis: target},
        device_id_type=pl.DeviceIdType.MESH,
    )


def loop(lo, hi, body):
    lax.fori_loop(lo, hi, lambda i, carry: (body(i), carry)[1], 0)


def hidden_kernel(
    n_seq, n_tp,
    tokens, out_grad, w_in, w_out,
    hidden_out, cols_out, input_grad,
    w_in_v, w_out_v, cols_in, cols, own,
    core_out, core_got, right_out, left_got, left_out, right_got,
    hidden, total, tp_got,
    w_sem, a2a_send, a2a_recv, core_send, core_recv,
    right_send, right_recv, left_send, left_recv,
    hid_send, hid_recv, tp_send, tp_recv, out_sem,
):
    seq, tp = lax.axis_index("seq"), lax.axis_index("tp")
    n_tok = cols.shape[1]
    feats = cols.shape[2]
    half = n_tok // 2
    wide = w_in_v.shape[2]
    n = CHUNKS
    chip, core = seq // 2, seq % 2
    last = n_seq // 2 - 1
    partner = chip * 2 + 1 - core
    right_dev = lax.rem(seq + 2, n_seq)
    left_dev = lax.rem(seq + n_seq - 2, n_seq)

    def w_copies(c):
        at = pl.ds(pl.multiple_of(c * wide, wide), wide)
        return (
            pltpu.make_async_copy(w_in.at[:, at], w_in_v.at[c], w_sem.at[0, c]),
            pltpu.make_async_copy(w_out.at[at, :], w_out_v.at[c], w_sem.at[1, c]),
        )

    def start_weights(c):
        for copy in w_copies(c):
            copy.start()

    loop(0, n, start_weights)

    barrier = pltpu.get_barrier_semaphore()

    def greet_seq(o):
        pl.semaphore_signal(barrier, inc=1, device_id={"seq": lax.rem(seq + o, n_seq)},
                            device_id_type=pl.DeviceIdType.MESH)

    def greet_tp(o):
        pl.semaphore_signal(barrier, inc=1, device_id={"tp": lax.rem(tp + o, n_tp)},
                            device_id_type=pl.DeviceIdType.MESH)

    loop(1, n_seq, greet_seq)
    loop(1, n_tp, greet_tp)
    pl.semaphore_wait(barrier, n_seq + n_tp - 2)

    def a2a(a, o):
        peer = lax.rem(seq + o, n_seq)
        src = (tokens, out_grad)[a]
        at = pl.ds(pl.multiple_of(peer * feats, feats), feats)
        return remote(src.at[:, at], cols_in.at[a, seq], a2a_send.at[a, peer],
                      a2a_recv.at[a, seq], "seq", peer)

    def a2a_arrival(a, o):
        peer = lax.rem(seq + o, n_seq)
        src = (tokens, out_grad)[a]
        at = pl.ds(pl.multiple_of(peer * feats, feats), feats)
        return remote(src.at[:, at], cols_in.at[a, peer], a2a_send.at[a, peer],
                      a2a_recv.at[a, peer], "seq", peer)

    def start_a2a(o):
        for a in range(2):
            a2a(a, o).start()

    loop(1, n_seq, start_a2a)
    mine = pl.ds(pl.multiple_of(seq * feats, feats), feats)
    cols_in[0, seq] = tokens[:, mine]
    cols_in[1, seq] = out_grad[:, mine]
    total[...] = jnp.zeros_like(total)

    @pl.when(chip == 0)
    def _():
        left_got[...] = jnp.zeros_like(left_got)

    @pl.when(chip == last)
    def _():
        right_got[...] = jnp.zeros_like(right_got)

    def wait_a2a(o):
        for a in range(2):
            a2a_arrival(a, o).wait_recv()

    loop(1, n_seq, wait_a2a)
    for a in range(2):
        cols[a] = cols_in[a].astype(F32).reshape(n_tok, feats).astype(BF16)

    def core_copy(c):
        return remote(core_out.at[c], core_got.at[c], core_send.at[c],
                      core_recv.at[c], "seq", partner)

    def right_copy(c):
        return remote(right_out.at[c], left_got.at[c], right_send.at[c],
                      right_recv.at[c], "seq", right_dev)

    def left_copy(c):
        return remote(left_out.at[c], right_got.at[c], left_send.at[c],
                      left_recv.at[c], "seq", left_dev)

    def hid_copy(c, which):
        part = hidden.at[c, which]
        return remote(part, part, hid_send.at[c], hid_recv.at[c], "seq", partner)

    def step(i):
        @pl.when(i < n)
        def _():
            for copy in w_copies(i):
                copy.wait()
            pre = jnp.dot(cols[0], w_in_v[i], preferred_element_type=F32)
            grad = lax.dot_general(cols[1], w_out_v[i], (((1,), (1,)), ((), ())),
                                   preferred_element_type=F32)
            for a, value in enumerate((pre, grad)):
                low, high = value[:half], value[half:]
                own[i, a] = jnp.where(core == 0, low, high)
                core_out[i, a] = jnp.where(core == 0, high, low).astype(BF16)
            core_copy(i).start()

        near = i - 1

        @pl.when((near >= 0) & (near < n))
        def _():
            core_copy(near).wait_recv()
            own[near] = own[near] + core_got[near].astype(F32)

        from_left = i - 1 - chip * LAG

        @pl.when((from_left >= 0) & (from_left < n))
        def _():
            @pl.when(chip > 0)
            def _():
                right_copy(from_left).wait_recv()

            @pl.when(chip < last)
            def _():
                right_out[from_left] = (
                    left_got[from_left].astype(F32) + own[from_left]
                ).astype(BF16)
                right_copy(from_left).start()

        from_right = i - 1 - (last - chip) * LAG

        @pl.when((from_right >= 0) & (from_right < n))
        def _():
            @pl.when(chip < last)
            def _():
                left_copy(from_right).wait_recv()

            @pl.when(chip > 0)
            def _():
                left_out[from_right] = (
                    right_got[from_right].astype(F32) + own[from_right]
                ).astype(BF16)
                left_copy(from_right).start()

        done = i - 1 - jnp.maximum(chip, last - chip) * LAG

        @pl.when((done >= 0) & (done < n))
        def _():
            value = own[done] + left_got[done].astype(F32) + right_got[done].astype(F32)
            posit = jnp.maximum(value[0], 0.0)
            hidden[done, core, 0] = (posit * posit).astype(BF16)
            hidden[done, core, 1] = (2.0 * posit * value[1]).astype(BF16)
            hid_copy(done, core).start()

        both = done - 1

        @pl.when((both >= 0) & (both < n))
        def _():
            hid_copy(both, 1 - core).wait_recv()
            slope = jnp.concatenate([hidden[both, 0, 1], hidden[both, 1, 1]], axis=0)
            part = lax.dot_general(slope, w_in_v[both], (((1,), (1,)), ((), ())),
                                   preferred_element_type=F32)
            total[...] += part.reshape(total.shape)

    loop(0, n + 2 + last * LAG, step)

    def tp_copy(o):
        peer = lax.rem(tp + o, n_tp)
        return remote(total.at[peer], tp_got.at[tp], tp_send.at[peer],
                      tp_recv.at[tp], "tp", peer)

    def tp_arrival(o):
        peer = lax.rem(tp + o, n_tp)
        return remote(total.at[peer], tp_got.at[peer], tp_send.at[peer],
                      tp_recv.at[peer], "tp", peer)

    loop(1, n_tp, lambda o: tp_copy(o).start())
    outs = (
        pltpu.make_async_copy(hidden, hidden_out, out_sem.at[0]),
        pltpu.make_async_copy(cols, cols_out, out_sem.at[1]),
    )
    for copy in outs:
        copy.start()

    def wait_sends(c):
        core_copy(c).wait_send()
        hid_copy(c, core).wait_send()

        @pl.when(chip < last)
        def _():
            right_copy(c).wait_send()

        @pl.when(chip > 0)
        def _():
            left_copy(c).wait_send()

    loop(0, n, wait_sends)

    def wait_a2a_sends(o):
        for a in range(2):
            a2a(a, o).wait_send()

    loop(1, n_seq, wait_a2a_sends)
    loop(1, n_tp, lambda o: tp_arrival(o).wait_recv())
    tp_got[tp] = total[tp]
    input_grad[...] = jnp.sum(tp_got[...], axis=0).astype(BF16)
    loop(1, n_tp, lambda o: tp_copy(o).wait_send())
    for copy in outs:
        copy.wait()


def grads_kernel(hidden, cols, grad_in, grad_out):
    act = jnp.concatenate([hidden[0, 0, 0], hidden[0, 1, 0]], axis=0)
    slope = jnp.concatenate([hidden[0, 0, 1], hidden[0, 1, 1]], axis=0)
    rows = (((0,), (0,)), ((), ()))
    grad_in[...] = lax.dot_general(cols[0], slope, rows, preferred_element_type=F32)
    grad_out[...] = lax.dot_general(act, cols[1], rows, preferred_element_type=F32)


def per_device(n_seq, n_tp, tokens, out_grad, w_in, w_out):
    n_tok = tokens.shape[0] * n_seq
    feats, units = w_in.shape
    wide = units // CHUNKS
    half = n_tok // 2
    n = CHUNKS
    vmem = pl.BlockSpec(memory_space=pltpu.VMEM)
    hbm = pl.BlockSpec(memory_space=pl.ANY)
    dma = pltpu.SemaphoreType.DMA
    pair = (n, 2, half, wide)
    hidden, cols, input_grad = pl.pallas_call(
        functools.partial(hidden_kernel, n_seq, n_tp),
        out_shape=(
            jax.ShapeDtypeStruct((n, 2, 2, half, wide), BF16),
            jax.ShapeDtypeStruct((2, n_tok, feats), BF16),
            jax.ShapeDtypeStruct((n_tok // n_tp, feats), BF16),
        ),
        in_specs=[vmem, vmem, hbm, hbm],
        out_specs=(hbm, hbm, vmem),
        scratch_shapes=[
            pltpu.VMEM((n, feats, wide), BF16),
            pltpu.VMEM((n, wide, feats), BF16),
            pltpu.VMEM((2, n_seq, tokens.shape[0], feats), BF16),
            pltpu.VMEM((2, n_tok, feats), BF16),
            pltpu.VMEM(pair, F32),
            pltpu.VMEM(pair, BF16),
            pltpu.VMEM(pair, BF16),
            pltpu.VMEM(pair, BF16),
            pltpu.VMEM(pair, BF16),
            pltpu.VMEM(pair, BF16),
            pltpu.VMEM(pair, BF16),
            pltpu.VMEM((n, 2, 2, half, wide), BF16),
            pltpu.VMEM((n_tp, n_tok // n_tp, feats), F32),
            pltpu.VMEM((n_tp, n_tok // n_tp, feats), F32),
            dma((2, n)),
            dma((2, n_seq)),
            dma((2, n_seq)),
            dma((n,)),
            dma((n,)),
            dma((n,)),
            dma((n,)),
            dma((n,)),
            dma((n,)),
            dma((n,)),
            dma((n,)),
            dma((n_tp,)),
            dma((n_tp,)),
            dma((2,)),
        ],
        compiler_params=pltpu.CompilerParams(
            collective_id=0, has_side_effects=True, vmem_limit_bytes=56 * 1024 * 1024
        ),
        name="hidden_exchange",
    )(tokens, out_grad, w_in, w_out)

    grad_in, grad_out = pl.pallas_call(
        grads_kernel,
        grid=(n,),
        out_shape=(
            jax.ShapeDtypeStruct((feats, units), F32),
            jax.ShapeDtypeStruct((units, feats), F32),
        ),
        in_specs=[
            pl.BlockSpec((1, 2, 2, half, wide), lambda c: (c, 0, 0, 0, 0)),
            pl.BlockSpec((2, n_tok, feats), lambda c: (0, 0, 0)),
        ],
        out_specs=(
            pl.BlockSpec((feats, wide), lambda c: (0, c)),
            pl.BlockSpec((wide, feats), lambda c: (c, 0)),
        ),
        name="weight_grads",
    )(hidden, cols)
    return input_grad, grad_in, grad_out


def solution(mesh):
    return jax.shard_map(
        functools.partial(per_device, mesh.shape["seq"], mesh.shape["tp"]),
        mesh=mesh,
        in_specs=(P("seq", None), P("seq", None), P("seq", "tp"), P("tp", "seq")),
        out_specs=(P("tp", "seq"), P("seq", "tp"), P("tp", "seq")),
        check_vma=False,
    )
```

time: 181 us -> 67.7 us (0.37)
  Pallas kernels: 0 us -> 65.3 us
  blocking collectives: 53.5 us -> 0 us
  waiting for transfers between devices: 53.3 us -> 0 us
  matrix products: 38.3 us -> 0 us
  local copies, waits for them, and re-layouts: 18.7 us -> 1.35 us
  between operations: 13.8 us -> 0.64 us
  other arithmetic: 2.47 us -> 0 us
    pallas_call x0 -> x2, Pallas kernels: none -> 65.3 us  [the longest x1 50.7 us: per_device(): pl.pallas_call(functools.partial(hidden_kernel, n_seq, n_tp), out_shape=(...]
    reduce_scatter x3 -> x0, waiting for transfers between devices: 53.3 us -> none  [the longest x1 35.5 us: per_device(): lax.psum_scatter(pre, 'seq', scatter_dimension=0, tiled=True)]
    dot_general x5 -> x0, matrix products: 38.3 us -> none  [the longest x2 16.6 us: over_rows(): lax.dot_general(left, right, (((0,), (0,)), ((), ())), preferred_element_...]
    all_gather x2 -> x0, blocking collectives: 32 us -> none  [the longest x1 16.2 us: per_device(): slope_piece = lax.all_gather(slope, 'seq', axis=0, tiled=True)]
    all_to_all x2 -> x0, blocking collectives: 21.5 us -> none  [the longest x1 12.7 us: per_device(): lax.all_to_all(out_grad, 'seq', split_axis=1, concat_axis=0, tiled=True)]
    unnamed x3 -> x1, local copies, waits for them, and re-layouts: 18.7 us -> 1.35 us
    convert_element_type x2 -> x0, other arithmetic: 2.47 us -> none  [the longest x1 1.41 us: per_device(): lax.psum_scatter(partial_value, 'tp', scatter_dimension=0, tiled=True)]
  transfers between devices with their start and end apart: 3 -> 0, of which waited for: 2 -> 0; matrix products, arithmetic and copies ran while one was open for 23% -> 0% of each run, Pallas kernels for 0% -> 0%
where the time goes in v1:
time: 67.7 us; the launch traced here: 67.3 us
  Pallas kernels  65.3 us (96%)
  local copies, waits for them, and re-layouts  1.35 us (2%)
    pallas_call x1, Pallas kernels, per_device(): pl.pallas_call(functools.partial(hidden_kernel, n_seq, n_tp), out_shape=(...  50.7 us
    pallas_call x1, Pallas kernels, per_device(): pl.pallas_call(grads_kernel, grid=(n,), out_shape=(jax.ShapeDtypeStruct((...  14.6 us

profile of v1, /device:TPU:0, one launch (start us, length us, event | category | flops | bytes accessed | tf_op | source)
XLA Modules:
  0.0 67.3 jit_solution(13328670212351866735)
XLA Ops:
  0.6 50.7 %hidden_exchange.1 = (bf16[12,2,2,32,512]{4,3,2,1,0:T(8,128)(2,1)}, bf16[2,64,768]{2,1,0:T(8,128)(2,1)}, bf16[16,768]{1,0:T(8,128)(2,1)}) custom-call(bf16[8,6144]{1,0:T(8,128)(2,1)} %tokens.1, bf16[8,6144]{1,0:T(8,128)(2,1)} %out_grad.1, bf16[768,6144]{1,0:T(8,128)(2,1)} %w_in.1, bf16[6144,768]{1,0:T(8,128)(2,1)} %w_out.1), custom_call_target="tpu_custom_call" | custom-call | tf_op jit(solution)/shard_map/hidden_exchange/pallas_call | solution.py:273
  51.3 14.6 %weight_grads.1 = (f32[768,6144]{1,0:T(8,128)}, f32[6144,768]{1,0:T(8,128)}) custom-call(bf16[12,2,2,32,512]{4,3,2,1,0:T(8,128)(2,1)} %get-tuple-element.9.hidden, bf16[2,64,768]{2,1,0:T(8,128)(2,1)} %get-tuple-element.10.cols), custom_call_target="tpu_custom_call" | custom-call | tf_op jit(solution)/shard_map/weight_grads/pallas_call | solution.py:318
  65.9 1.3 %copy.8 = bf16[16,768]{1,0:T(8,128)(2,1)} copy(bf16[16,768]{1,0:T(8,128)(2,1)} %get-tuple-element.16) | data formatting | bytes 49152

commit v2 on v1

--- a/solution.py
+++ b/solution.py
@@ -7,8 +7,10 @@
 from jax.experimental.pallas import tpu as pltpu
 from jax.sharding import PartitionSpec as P
 
-CHUNKS = 12
-LAG = 2
+MOST_CHUNKS = 24
+LAG = 5
+CORE_LAG = 3
+HID_LAG = 3
 F32 = jnp.float32
 BF16 = jnp.bfloat16
 
@@ -44,7 +46,7 @@
     feats = cols.shape[2]
     half = n_tok // 2
     wide = w_in_v.shape[2]
-    n = CHUNKS
+    n = w_in_v.shape[0]
     chip, core = seq // 2, seq % 2
     last = n_seq // 2 - 1
     partner = chip * 2 + 1 - core
@@ -148,14 +150,14 @@
                 core_out[i, a] = jnp.where(core == 0, high, low).astype(BF16)
             core_copy(i).start()
 
-        near = i - 1
+        near = i - CORE_LAG
 
         @pl.when((near >= 0) & (near < n))
         def _():
             core_copy(near).wait_recv()
             own[near] = own[near] + core_got[near].astype(F32)
 
-        from_left = i - 1 - chip * LAG
+        from_left = i - CORE_LAG - chip * LAG
 
         @pl.when((from_left >= 0) & (from_left < n))
         def _():
@@ -170,7 +172,7 @@
                 ).astype(BF16)
                 right_copy(from_left).start()
 
-        from_right = i - 1 - (last - chip) * LAG
+        from_right = i - CORE_LAG - (last - chip) * LAG
 
         @pl.when((from_right >= 0) & (from_right < n))
         def _():
@@ -185,7 +187,7 @@
                 ).astype(BF16)
                 left_copy(from_right).start()
 
-        done = i - 1 - jnp.maximum(chip, last - chip) * LAG
+        done = i - CORE_LAG - jnp.maximum(chip, last - chip) * LAG
 
         @pl.when((done >= 0) & (done < n))
         def _():
@@ -195,7 +197,7 @@
             hidden[done, core, 1] = (2.0 * posit * value[1]).astype(BF16)
             hid_copy(done, core).start()
 
-        both = done - 1
+        both = done - HID_LAG
 
         @pl.when((both >= 0) & (both < n))
         def _():
@@ -205,7 +207,7 @@
                                    preferred_element_type=F32)
             total[...] += part.reshape(total.shape)
 
-    loop(0, n + 2 + last * LAG, step)
+    loop(0, n + CORE_LAG + HID_LAG + last * LAG, step)
 
     def tp_copy(o):
         peer = lax.rem(tp + o, n_tp)
@@ -252,9 +254,18 @@
         copy.wait()
 
 
-def grads_kernel(hidden, cols, grad_in, grad_out):
-    act = jnp.concatenate([hidden[0, 0, 0], hidden[0, 1, 0]], axis=0)
-    slope = jnp.concatenate([hidden[0, 0, 1], hidden[0, 1, 1]], axis=0)
+def grads_kernel(hidden, cols, given, input_grad, grad_in, grad_out):
+    input_grad[...] = given[...]
+    act, slope = (
+        jnp.concatenate(
+            [
+                jnp.concatenate([hidden[g, 0, a], hidden[g, 1, a]], axis=0)
+                for g in range(hidden.shape[0])
+            ],
+            axis=1,
+        )
+        for a in range(2)
+    )
     rows = (((0,), (0,)), ((), ()))
     grad_in[...] = lax.dot_general(cols[0], slope, rows, preferred_element_type=F32)
     grad_out[...] = lax.dot_general(act, cols[1], rows, preferred_element_type=F32)
@@ -263,9 +274,10 @@
 def per_device(n_seq, n_tp, tokens, out_grad, w_in, w_out):
     n_tok = tokens.shape[0] * n_seq
     feats, units = w_in.shape
-    wide = units // CHUNKS
+    wide = max(128, units // MOST_CHUNKS)
     half = n_tok // 2
-    n = CHUNKS
+    n = units // wide
+    group = next(g for g in (4, 3, 2, 1) if n % g == 0)
     vmem = pl.BlockSpec(memory_space=pltpu.VMEM)
     hbm = pl.BlockSpec(memory_space=pl.ANY)
     dma = pltpu.SemaphoreType.DMA
@@ -315,24 +327,27 @@
         name="hidden_exchange",
     )(tokens, out_grad, w_in, w_out)
 
-    grad_in, grad_out = pl.pallas_call(
+    whole = pl.BlockSpec((n_tok // n_tp, feats), lambda c: (0, 0))
+    return pl.pallas_call(
         grads_kernel,
-        grid=(n,),
+        grid=(n // group,),
         out_shape=(
+            jax.ShapeDtypeStruct((n_tok // n_tp, feats), BF16),
             jax.ShapeDtypeStruct((feats, units), F32),
             jax.ShapeDtypeStruct((units, feats), F32),
         ),
         in_specs=[
-            pl.BlockSpec((1, 2, 2, half, wide), lambda c: (c, 0, 0, 0, 0)),
+            pl.BlockSpec((group, 2, 2, half, wide), lambda c: (c, 0, 0, 0, 0)),
             pl.BlockSpec((2, n_tok, feats), lambda c: (0, 0, 0)),
+            whole,
         ],
         out_specs=(
-            pl.BlockSpec((feats, wide), lambda c: (0, c)),
-            pl.BlockSpec((wide, feats), lambda c: (c, 0)),
+            whole,
+            pl.BlockSpec((feats, group * wide), lambda c: (0, c)),
+            pl.BlockSpec((group * wide, feats), lambda c: (c, 0)),
         ),
         name="weight_grads",
-    )(hidden, cols)
-    return input_grad, grad_in, grad_out
+    )(hidden, cols, input_grad)
 
 
 def solution(mesh):

time: 67.7 us -> 62.6 us (0.925)
  Pallas kernels: 65.3 us -> 61.8 us
  local copies, waits for them, and re-layouts: 1.35 us -> 0 us
    pallas_call x1, Pallas kernels: 50.7 us -> 47.7 us  [per_device(): pl.pallas_call(functools.partial(hidden_kernel, n_seq, n_tp), out_shape=(...]
    unnamed x1 -> x0, local copies, waits for them, and re-layouts: 1.35 us -> none
where the time goes in v2:
time: 62.6 us; the launch traced here: 62.4 us
  Pallas kernels  61.8 us (99%)
  between operations  0.64 us (1%)
    pallas_call x1, Pallas kernels, per_device(): pl.pallas_call(functools.partial(hidden_kernel, n_seq, n_tp), out_shape=(...  47.7 us
    pallas_call x1, Pallas kernels, per_device(): pl.pallas_call(grads_kernel, grid=(n // group,), out_shape=(jax.ShapeDtyp...  14 us

profile of v2, /device:TPU:0, one launch (start us, length us, event | category | flops | bytes accessed | tf_op | source)
XLA Modules:
  0.0 62.4 jit_solution(3353389045871798063)
XLA Ops:
  0.6 47.7 %hidden_exchange.1 = (bf16[24,2,2,32,256]{4,3,2,1,0:T(8,128)(2,1)}, bf16[2,64,768]{2,1,0:T(8,128)(2,1)}, bf16[16,768]{1,0:T(8,128)(2,1)}) custom-call(bf16[8,6144]{1,0:T(8,128)(2,1)} %tokens.1, bf16[8,6144]{1,0:T(8,128)(2,1)} %out_grad.1, bf16[768,6144]{1,0:T(8,128)(2,1)} %w_in.1, bf16[6144,768]{1,0:T(8,128)(2,1)} %w_out.1), custom_call_target="tpu_custom_call" | custom-call | tf_op jit(solution)/shard_map/hidden_exchange/pallas_call | solution.py:285
  48.4 14.0 %weight_grads.1 = (bf16[16,768]{1,0:T(8,128)(2,1)}, f32[768,6144]{1,0:T(8,128)}, f32[6144,768]{1,0:T(8,128)}) custom-call(bf16[24,2,2,32,256]{4,3,2,1,0:T(8,128)(2,1)} %get-tuple-element.6.hidden, bf16[2,64,768]{2,1,0:T(8,128)(2,1)} %get-tuple-element.7.cols, bf16[16,768]{1,0:T(8,128)(2,1)} %get-tuple-element.8.given), custom_call_target="tpu_custom_call" | custom-call | tf_op jit(solution)/shard_map/weight_grads/pallas_call | solution.py:331
